TPU v7x, 32 devices: a whole 2x2x4 slice. The times are simulated.
32 devices in a mesh: groups: 2 (over x), fsdp: 16 (over z, y, core).
Axes of the slice: x: 2, y: 2, z: 4, core: 2. Of those that a mesh axis runs over, the one named last changes fastest.
Arguments:
- obs_feat: bfloat16 [12288, 2048], P(('groups', 'fsdp')), parts along dimension 0, may hold values from -6 to 6
- reward: float32 [512, 24], P(('groups', 'fsdp')), parts along dimension 0, may hold values from -22 to 22
- value_old: float32 [512, 25], P(('groups', 'fsdp')), parts along dimension 0, may hold values from -6 to 6
- done: int32 [512, 24], P(('groups', 'fsdp')), parts along dimension 0, may hold values 0 or 1
- minibatch_perm: int32 [12288], P(('groups', 'fsdp')), parts along dimension 0, may hold values from 0 to 6143, as said below
- old_mean: bfloat16 [12288, 12], P(('groups', 'fsdp')), parts along dimension 0, may hold values from -6 to 6
- noise: bfloat16 [12288, 12], P(('groups', 'fsdp')), parts along dimension 0, may hold values from -6 to 6
- gain_in: float32 [2048], replicated, may hold values from 0.5 to 1.5
- out_weight: bfloat16 [2048, 2048], P('fsdp'), may hold values from -0.125 to 0.125
- head_weight: bfloat16 [2048, 13], replicated, may hold values from -0.125 to 0.125
- log_std: float32 [12], replicated, may hold values from 0.7 to 1.3
Outputs:
- hidden_out: bfloat16 [12288, 2048], P(('groups', 'fsdp')), parts along dimension 0
- grad_weight: float32 [4096, 2048], P(('groups', 'fsdp')), parts along dimension 0
- grad_head: float32 [4096, 13], P('groups'), parts along dimension 0
- grad_std: float32 [24], P('groups'), parts along dimension 0
There are 2 independent parts, one for each index of `groups`. A program takes and returns all parts, laid end to end along the dimension named above; an argument that names none is the same for every part. Nothing has to cross between parts.
Inputs may be any that keep to these rules, and one draw needn't show every extreme that they name: `minibatch_perm`: rows of one index of fsdp go 24 to each index of fsdp; the block of 384 minibatch positions of index j holds at positions j * 384 + s * 24 + c the rows from index s; a permutation of all rows.
All inputs are finite; a program needn't handle non-finite values. No bound on the sum of `done` on one device may be relied on, other than what follows from the above.
Results may differ from a plain program's by a relative error of at most 0.0095.
Values may be sent and summed in bfloat16 or wider, within the bound.
A program may use at most 128 MiB of HBM per device.

v0:
```python
import jax
import jax.numpy as jnp
from jax import lax
from jax.sharding import PartitionSpec as P

GAMMA = 0.99
LAMBDA_GAE = 0.95
CLIP_EPS = 0.2
NORM_EPS = 1e-05


def advantages(reward, value_old, done):
    keep = 1.0 - done.astype(jnp.float32)
    deltas = reward + GAMMA * value_old[:, 1:] * keep - value_old[:, :-1]

    def walk(carry, inputs):
        dstep, kstep = inputs
        carry = dstep + GAMMA * LAMBDA_GAE * kstep * carry
        return (carry, carry)

    start = jnp.zeros((reward.shape[0],), jnp.float32)
    _, stacked = lax.scan(walk, start, (deltas.T, keep.T), reverse=True)
    gae = stacked.T
    return (gae.reshape(-1), (gae + value_old[:, :-1]).reshape(-1))


def compute_rows(
    rows_x, old_mean, noise, adv_b, ret_b, gain_in, out_weight, head_weight, log_std, scale
):
    xf = rows_x.astype(jnp.float32)
    normed = (xf * lax.rsqrt(jnp.mean(xf * xf, -1, keepdims=True) + NORM_EPS) * gain_in).astype(
        jnp.bfloat16
    )
    columns = normed
    hidden = xf + jnp.dot(
        columns,
        lax.all_gather(out_weight, "fsdp", axis=0, tiled=True),
        preferred_element_type=jnp.float32,
    )
    rinv = lax.rsqrt(jnp.mean(hidden * hidden, -1, keepdims=True) + NORM_EPS)
    hnorm = hidden * rinv
    hnorm_b = hnorm.astype(jnp.bfloat16)
    heads = jnp.dot(hnorm_b, head_weight, preferred_element_type=jnp.float32)
    nact = log_std.shape[0]
    mean_act = heads[:, :nact]
    value = heads[:, nact]
    std_dev = jnp.exp(log_std)
    offset = old_mean.astype(jnp.float32) - mean_act
    sample = noise.astype(jnp.float32)
    logr = jnp.sum(-sample * offset / std_dev - offset * offset / (2.0 * std_dev * std_dev), -1)
    ratio = jnp.exp(logr)
    advant = adv_b.astype(jnp.float32)
    clipped = jnp.clip(ratio, 1.0 - CLIP_EPS, 1.0 + CLIP_EPS)
    active = ratio * advant <= clipped * advant
    gratio = jnp.where(active, -scale * advant, 0.0)
    glogr = gratio * ratio
    gmean = glogr[:, None] * (sample / std_dev + offset / (std_dev * std_dev))
    gvalue = scale * (value - ret_b.astype(jnp.float32))
    std_local = jnp.sum(
        glogr[:, None] * (sample * offset / std_dev + offset * offset / (std_dev * std_dev)), 0
    )
    ghead = jnp.concatenate([gmean, gvalue[:, None]], 1)
    head_local = jnp.dot(hnorm_b.astype(jnp.float32).T, ghead, precision=lax.Precision.HIGHEST)
    ghn = jnp.dot(ghead, head_weight.astype(jnp.float32).T, precision=lax.Precision.HIGHEST)
    ghid = rinv * (ghn - hnorm * jnp.mean(ghn * hnorm, -1, keepdims=True))
    ghid_b = ghid.astype(jnp.bfloat16)
    columns = normed
    grad_weight = lax.psum_scatter(
        lax.dot_general(
            columns, ghid_b, (((0,), (0,)), ((), ())), preferred_element_type=jnp.float32
        ),
        "fsdp",
        scatter_dimension=0,
        tiled=True,
    )
    grad_head, grad_std = lax.psum((head_local, std_local), "fsdp")
    return (hidden.astype(jnp.bfloat16), grad_weight, grad_head, grad_std)


def local(
    obs_feat,
    reward,
    value_old,
    done,
    minibatch_perm,
    old_mean,
    noise,
    gain_in,
    out_weight,
    head_weight,
    log_std,
):
    gae, returns = advantages(reward, value_old, done)
    local_rows = obs_feat.shape[0]
    devices = lax.axis_size("fsdp")
    total_rows = local_rows * devices
    sums, squares = lax.psum((jnp.sum(gae), jnp.sum(gae * gae)), "fsdp")
    mean_adv = sums / total_rows
    var_adv = squares / total_rows - mean_adv * mean_adv
    adv_b = ((gae - mean_adv) * lax.rsqrt(var_adv + NORM_EPS)).astype(jnp.bfloat16)
    ret_b = returns.astype(jnp.bfloat16)
    scale = 1.0 / jnp.sqrt(jnp.float32(total_rows))
    per_peer = local_rows // devices
    send_slot = minibatch_perm // local_rows * per_peer + minibatch_perm % per_peer
    hidden_local, grad_weight, grad_head, grad_std = compute_rows(
        obs_feat, old_mean, noise, adv_b, ret_b, gain_in, out_weight, head_weight, log_std, scale
    )
    send_hidden = jnp.zeros_like(hidden_local).at[send_slot].set(hidden_local)
    hidden_out = lax.all_to_all(send_hidden, "fsdp", split_axis=0, concat_axis=0, tiled=True)
    return (hidden_out, grad_weight, grad_head, grad_std)


def solution(mesh):
    return jax.shard_map(
        local,
        mesh=mesh,
        in_specs=(
            P(("groups", "fsdp"), None),
            P(("groups", "fsdp"), None),
            P(("groups", "fsdp"), None),
            P(("groups", "fsdp"), None),
            P(("groups", "fsdp")),
            P(("groups", "fsdp"), None),
            P(("groups", "fsdp"), None),
            P(),
            P("fsdp", None),
            P(),
            P(),
        ),
        out_specs=(
            P(("groups", "fsdp"), None),
            P(("groups", "fsdp"), None),
            P("groups", None),
            P("groups"),
        ),
        check_vma=False,
    )
```

profile of v0, /device:TPU:9, one launch (start us, length us, event | category | flops | bytes accessed | tf_op | source)
XLA Modules:
  0.0 386.5 jit_solution(8685224248298809231)
XLA Ops:
  7.2 0.0 copy-start
  7.2 0.0 all-gather.2.cloned.1.call-start
  7.2 0.7 all-gather.2.cloned.1.call-update
  7.9 0.0 all-reduce.3.cloned.1.call-start
  8.0 0.9 fusion.31
  8.8 0.1 copy.26
  8.9 0.1 copy.27
  9.0 1.8 while.17
  10.8 0.1 copy.28
  10.8 0.6 fusion.29
  11.5 0.6 reduce_sum.66
  12.1 25.2 %all-reduce = (f32[]{:T(128)}, f32[]{:T(128)}) all-reduce(f32[]{:T(128)} %fusion.29, f32[]{:T(128)} %reduce_sum.66), channel_id=1, replica_groups=mesh['groups'=2,'fsdp'=16] {'fsdp'}, use_global_device_ids=true, to_apply=%region_9.10 | all-reduce | flops 2 | bytes 16 | tf_op jit(solution)/shard_map/psum | solution.py:97
  39.9 0.7 fusion.33
  40.6 0.1 reshape.79
  40.7 0.1 reshape.80
  40.8 1.8 fusion.2
  42.6 0.7 fusion.39
  43.2 42.8 %all-gather.2.cloned.1.call-done = bf16[2048,2048]{1,0:T(8,128)(2,1)} async-done(((bf16[128,2048]{1,0:T(8,128)(2,1)}), bf16[2048,2048]{1,0:T(8,128)(2,1)}) %all-gather.2.cloned.1.call-update) | async-done | bytes 8388624 | tf_op jit(solution)/shard_map/all_gather | solution.py:37
  86.1 7.9 %multiply_reduce_fusion.1 = (f32[384]{0:T(512)S(1)}, f32[384,2048]{1,0:T(8,128)S(1)}) fusion(bf16[2048,2048]{1,0:T(8,128)(2,1)} %all-gather.2.cloned.1.call-done, bf16[384,2048]{1,0:T(8,128)(2,1)} %param.13, f32[2048]{0:T(1024)} %param.20, f32[384]{0:T(512)S(1)} %add_rsqrt_fusion.1), kind=kOutput, calls=%fused_computation.12 | convolution fusion | flops 3227516416 | bytes 13118464 | tf_op jit(solution)/shard_map/dot_general | solution.py:35
  93.9 0.0 copy-start.2
  93.9 0.0 copy-start.3
  94.0 0.2 multiply_convert_fusion.1
  94.2 0.0 copy-done
  94.2 0.5 fusion.40
  94.7 0.0 copy-done.2
  94.7 0.0 copy-done.3
  94.8 0.1 fusion.23
  94.9 0.2 fusion.24
  95.1 0.0 copy-start.4
  95.1 3.4 multiply_reduce_fusion
  98.4 1.4 fusion.25
  99.8 0.0 all-reduce.3.cloned.1.call-update
  99.8 0.2 reduce-scatter.2.cloned.1.call-start
  100.1 0.0 copy-done.4
  100.1 12.9 %fusion.5 = f32[2048,2048]{1,0:T(8,128)} fusion(f32[384,2048]{1,0:T(8,128)} %get-tuple-element.155, f32[384,2048]{1,0:T(8,128)S(1)} %get-tuple-element.153, f32[384]{0:T(512)S(1)} %broadcast_multiply_fusion, f32[384]{0:T(512)S(1)} %add_rsqrt_fusion, bf16[384,2048]{1,0:T(8,128)(2,1)} %param.13, f32[2048]{0:T(1024)S(1)} %copy-done.4, f32[384]{0:T(512)S(1)} %add_rsqrt_fusion.1), kind=kOutput, calls=%fused_computation.14 | convolution fusion | flops 3228303360 | bytes 24654336 | tf_op jit(solution)/shard_map/dot_general | solution.py:69
  113.0 0.0 copy-start.5
  113.0 0.0 reduce-scatter.2.cloned.1.call-update
  113.0 0.7 copy-done.5
  113.7 4.1 %scatter_custom_fusion = bf16[384,2048]{1,0:T(8,128)(2,1)} fusion(s32[384]{0:T(512)S(1)} %compare_select_fusion, f32[384,2048]{1,0:T(8,128)S(1)} %get-tuple-element.153, bf16[]{:T(256)} %constant.88.clone.1), kind=kCustom, calls=%fused_computation.17 | custom fusion | flops 786432 | bytes 4718594 | tf_op jit(solution)/shard_map/scatter | solution.py:108
  117.8 4.2 %all-to-all-start = ((bf16[16,24,2048]{2,1,0:T(8,128)(2,1)}), bf16[16,24,2048]{2,1,0:T(8,128)(2,1)S(1)}, u32[]{:S(2)}, u32[]{:S(2)}) async-start(bf16[16,24,2048]{2,1,0:T(8,128)(2,1)} %bitcast.39), calls=%async_computation | async-start | bytes 3145728 | tf_op jit(solution)/shard_map/all_to_all | solution.py:109
  122.0 52.4 %psum.31 = f32[12]{0:T(128)} all-reduce(f32[12]{0:T(128)S(1)} %get-tuple-element.143), channel_id=1, replica_groups=mesh['groups'=2,'fsdp'=16] {'fsdp'}, use_global_device_ids=true, to_apply=%region_14.15 | all-reduce | flops 12 | bytes 96 | tf_op jit(solution)/shard_map/psum | solution.py:76
  174.3 0.0 all-to-all-done
  174.3 20.8 %all-reduce.3.cloned.1.call-done = f32[2048,13]{0,1:T(8,128)} async-done(((f32[2048,13]{0,1:T(8,128)}), f32[2048,13]{0,1:T(8,128)}) %all-reduce.3.cloned.1.call-update) | async-done | bytes 106512 | tf_op jit(solution)/shard_map/psum | solution.py:76
  195.2 0.0 copy-start.1
  195.2 182.9 %reduce-scatter.2.cloned.1.call-done = f32[128,2048]{1,0:T(8,128)} async-done(((f32[2048,2048]{1,0:T(8,128)}), f32[128,2048]{1,0:T(8,128)}) %reduce-scatter.2.cloned.1.call-update) | async-done | bytes 1048592 | tf_op jit(solution)/shard_map/reduce_scatter | solution.py:68
  378.1 1.1 copy.41
  379.3 0.0 copy-done.1
  379.3 0.7 copy.42
  (56 shorter events, 1.5 us)
Async XLA Ops:
  7.2 87.0 %copy-start = (bf16[2048,13]{0,1:T(8,128)(2,1)S(1)}, bf16[2048,13]{0,1:T(8,128)(2,1)}, u32[]{:S(2)}) copy-start(bf16[2048,13]{0,1:T(8,128)(2,1)} %param.22) | copy-start | bytes 159748
  7.2 78.9 %all-gather.2.cloned.1.call-start = ((), (), s32[]{:S(2)}) async-start(), calls=%async_computation.2 | async-start | bytes 8912896 | tf_op jit(solution)/shard_map/all_gather | solution.py:37
  7.9 187.3 %all-reduce.3.cloned.1.call-start = ((), (), s32[]{:S(2)}) async-start(), calls=%async_computation.4 | async-start | bytes 262144 | tf_op jit(solution)/shard_map/psum | solution.py:76
  93.9 0.8 copy-start.2
  93.9 0.8 copy-start.3
  95.1 5.0 %copy-start.4 = (f32[2048]{0:T(1024)S(1)}, f32[2048]{0:T(1024)}, u32[]{:S(2)}) copy-start(f32[2048]{0:T(1024)} %param.20) | copy-start | bytes 24580
  99.8 278.3 %reduce-scatter.2.cloned.1.call-start = ((), (), s32[]{:S(2)}) async-start(), calls=%async_computation.3 | async-start | bytes 17825792 | tf_op jit(solution)/shard_map/reduce_scatter | solution.py:68
  113.0 0.7 copy-start.5
  117.8 56.6 %all-to-all-start = ((bf16[16,24,2048]{2,1,0:T(8,128)(2,1)}), bf16[16,24,2048]{2,1,0:T(8,128)(2,1)S(1)}, u32[]{:S(2)}, u32[]{:S(2)}) async-start(bf16[16,24,2048]{2,1,0:T(8,128)(2,1)} %bitcast.39), calls=%async_computation | async-start | bytes 3145728 | tf_op jit(solution)/shard_map/all_to_all | solution.py:109
  195.2 184.1 %copy-start.1 = (f32[2048,13]{0,1:T(8,128)S(1)}, f32[2048,13]{0,1:T(8,128)}, u32[]{:S(2)}) copy-start(f32[2048,13]{0,1:T(8,128)} %all-reduce.3.cloned.1.call-done) | copy-start | bytes 319492
Sparse Core Ops, SparseCore 0:
  10.2 75.8 all-gather.1
  100.0 95.1 all-reduce.2
  199.9 178.2 reduce-scatter.1
where the time goes:
time: 390 us; the launch traced here: 386 us
  waiting for transfers between devices  247 us (63%)
  blocking collectives  77.6 us (20%)
  matrix products  26 us (7%)
  between operations  16.5 us (4%)
  other arithmetic  10.4 us (3%)
  starting transfers between devices  4.48 us (1%)
    reduce_scatter x1, waiting for transfers between devices, compute_rows(): lax.psum_scatter(lax.dot_general(columns, ghid_b, (((0,), (0,)), ((), ())...  183 us
    psum x1, blocking collectives, compute_rows(): grad_head, grad_std = lax.psum((head_local, std_local), 'fsdp')  52.4 us
    all_gather x1, waiting for transfers between devices, compute_rows(): lax.all_gather(out_weight, 'fsdp', axis=0, tiled=True)  42.8 us
    psum x1, blocking collectives, local(): sums, squares = lax.psum((jnp.sum(gae), jnp.sum(gae * gae)), 'fsdp')  25.2 us
    psum x1, waiting for transfers between devices, compute_rows(): grad_head, grad_std = lax.psum((head_local, std_local), 'fsdp')  20.8 us
    dot_general x1, matrix products, compute_rows(): lax.dot_general(columns, ghid_b, (((0,), (0,)), ((), ())), preferred_elem...  12.9 us
    dot_general x1, matrix products, compute_rows(): jnp.dot(columns, lax.all_gather(out_weight, 'fsdp', axis=0, tiled=True),...  7.86 us
  transfers between devices with their start and end apart: 4, of which 3 were waited for; matrix products, arithmetic and copies ran while one was open for 6% of the time, Pallas kernels for 0%

commit v1 on v0

v1 whole, which is shorter than its diff:
```python
import functools

import jax
import jax.numpy as jnp
from jax import lax
from jax.experimental import pallas as pl
from jax.experimental.pallas import tpu as pltpu
from jax.sharding import PartitionSpec as P

GAMMA = 0.99
LAMBDA_GAE = 0.95
CLIP_EPS = 0.2
NORM_EPS = 1e-05
MESH = pl.DeviceIdType.MESH
TILE = 512


def chip_at(pos, ring):
    half = ring // 2
    col = pos // half
    row = col * (ring - 1 - pos) + (1 - col) * pos
    return 2 * row + col


class Ring:
    def __init__(self, n):
        self.n = n
        self.me = lax.axis_index("fsdp")
        self.ring = n // 2
        self.core = lax.rem(self.me, 2)
        chip = self.me // 2
        col = lax.rem(chip, 2)
        row = chip // 2
        self.pos = col * (self.ring - 1 - row) + (1 - col) * row
        self.step = 1 - 2 * self.core
        self.sibling = self.me + self.step

    def device(self, ahead, core):
        pos = lax.rem(self.pos + ahead + self.ring, self.ring)
        return 2 * chip_at(pos, self.ring) + core

    def down(self):
        return self.device(self.step, self.core)


def enter(n, me):
    barrier = pltpu.get_barrier_semaphore()

    @pl.loop(1, n)
    def _(k):
        pl.semaphore_signal(
            barrier, inc=1, device_id={"fsdp": lax.rem(me + k, n)}, device_id_type=MESH
        )

    pl.semaphore_wait(barrier, n - 1)


def remote(src, dst, send, recv, device):
    return pltpu.make_async_remote_copy(
        src_ref=src,
        dst_ref=dst,
        send_sem=send,
        recv_sem=recv,
        device_id={"fsdp": device},
        device_id_type=MESH,
    )


def pieces(rows):
    count = 2 if rows % 32 == 0 else 1
    return [pl.ds(i * (rows // count), rows // count) for i in range(count)]


def spread(n, me, source_of, dst, send, recv):
    @pl.loop(1, n)
    def _(k):
        peer = lax.rem(me + k, n)
        remote(source_of(peer), dst.at[me], send, recv, peer).start()


def collect(n, slots, sem):
    part = slots.at[pl.ds(0, n - 1)]
    pltpu.make_async_copy(part, part, sem).wait()


def forward_kernel(
    n, x_ref, normed_ref, stat_ref, w_ref, hidden_ref, sums_ref,
    held, stats, local_sem, ring_send, ring_recv, sib_send, sib_recv, stat_send, stat_recv,
):
    r = Ring(n)
    me, last = r.me, r.ring - 1
    own = pltpu.make_async_copy(w_ref, held.at[me], local_sem)
    own.start()
    enter(n, me)
    cuts = pieces(held.shape[1])
    down = r.down()

    def ring_copy(owner, step, i):
        part = held.at[owner, cuts[i]]
        return remote(part, part, ring_send.at[step, i], ring_recv.at[step, i], down)

    def sib_copy(owner, step, i):
        part = held.at[owner, cuts[i]]
        return remote(part, part, sib_send.at[step, i], sib_recv.at[step, i], r.sibling)

    def mine(step):
        return r.device(-r.step * step, r.core)

    def theirs(step):
        return r.device(r.step * step, 1 - r.core)

    def add(owner):
        for j in range(0, hidden_ref.shape[1], TILE):
            cols = pl.ds(j, TILE)
            hidden_ref[:, cols] += jnp.dot(
                normed_ref[owner], held[owner, :, cols], preferred_element_type=jnp.float32
            )

    own.wait()
    for i in range(len(cuts)):
        ring_copy(me, 1, i).start()
        sib_copy(me, 0, i).start()
    spread(n, me, lambda peer: stat_ref, stats, stat_send, stat_recv)
    stats[me] = stat_ref[...]
    hidden_ref[...] = x_ref[...].astype(jnp.float32)

    def hop(step, _):
        owner = mine(step)
        for i in range(len(cuts)):
            ring_copy(owner, step, i).wait_recv()

            @pl.when(step < last)
            def _():
                ring_copy(owner, step + 1, i).start()

            sib_copy(owner, step, i).start()
            if i == 0:
                add(mine(step - 1))
        for i in range(len(cuts)):
            sib_copy(theirs(step - 1), step - 1, i).wait_recv()
        add(theirs(step - 1))
        return 0

    lax.fori_loop(1, r.ring, hop, 0)
    add(mine(last))
    for i in range(len(cuts)):
        sib_copy(theirs(last), last, i).wait_recv()
    add(theirs(last))
    collect(n, stats, stat_recv)
    sums_ref[...] = jnp.sum(stats[...], 0)
    collect(n, stats, stat_send)

    def drain(step, _):
        owner = mine(step)
        for i in range(len(cuts)):
            @pl.when(step < last)
            def _():
                ring_copy(owner, step + 1, i).wait_send()

            sib_copy(owner, step, i).wait_send()
        return 0

    lax.fori_loop(0, r.ring, drain, 0)


def forward(n, x, normed, stat, weight):
    rows, width = x.shape
    shard = weight.shape[0]
    blocks = normed.reshape(rows, n, shard).transpose(1, 0, 2)
    count = len(pieces(shard))
    vmem = pl.BlockSpec(memory_space=pltpu.VMEM)
    sems = pltpu.SemaphoreType.DMA
    return pl.pallas_call(
        functools.partial(forward_kernel, n),
        name="forward",
        out_shape=(
            jax.ShapeDtypeStruct((rows, width), jnp.float32),
            jax.ShapeDtypeStruct(stat.shape, jnp.float32),
        ),
        in_specs=[vmem, vmem, vmem, pl.BlockSpec(memory_space=pl.ANY)],
        out_specs=(vmem, vmem),
        scratch_shapes=[
            pltpu.VMEM((n, shard, width), jnp.bfloat16),
            pltpu.VMEM((n,) + stat.shape, jnp.float32),
            sems(()),
            sems((n // 2, count)),
            sems((n // 2, count)),
            sems((n // 2, count)),
            sems((n // 2, count)),
            sems(()),
            sems(()),
        ],
        compiler_params=pltpu.CompilerParams(
            collective_id=0, has_side_effects=True, vmem_limit_bytes=60 << 20
        ),
        cost_estimate=pl.CostEstimate(
            flops=2 * rows * width * width, bytes_accessed=16 * rows * width, transcendentals=0
        ),
    )(x, blocks, stat, weight)


def backward_kernel(
    n, normed_ref, ghid_ref, head_ref, grad_ref, heads_ref,
    own, sib_out, sib_in, ring_out, ring_in, head_in, head_sum, head_all,
    ring_send, ring_recv, sib_send, sib_recv, head_sems,
):
    r = Ring(n)
    me, last = r.me, r.ring - 1
    enter(n, me)
    width = grad_ref.shape[1]
    cuts = pieces(grad_ref.shape[0])
    down = r.down()

    def product(owner, cols):
        return lax.dot_general(
            normed_ref[owner],
            ghid_ref[:, cols],
            (((0,), (0,)), ((), ())),
            preferred_element_type=jnp.float32,
        )

    def ring_copy(step, i):
        return remote(
            ring_out.at[step, cuts[i]], ring_in.at[step, cuts[i]],
            ring_send.at[step, i], ring_recv.at[step, i], down,
        )

    def sib_copy(step):
        return remote(
            sib_out.at[step], sib_in.at[step], sib_send.at[step], sib_recv.at[step], r.sibling
        )

    def terms(step):
        theirs = r.device(-r.step * (last - step), 1 - r.core)
        for j in range(0, width, TILE):
            cols = pl.ds(j, TILE)
            sib_out[step, :, cols] = product(theirs, cols).astype(jnp.bfloat16)
        sib_copy(step).start()
        mine = r.device(r.step * (last - step), r.core)
        for j in range(0, width, TILE):
            cols = pl.ds(j, TILE)
            own[:, cols] = product(mine, cols)
        sib_copy(step).wait_recv()

    terms(0)
    for i, cut in enumerate(cuts):
        ring_out[0, cut] = (own[cut] + sib_in[0, cut].astype(jnp.float32)).astype(jnp.bfloat16)
        ring_copy(0, i).start()
    spread(n, me, lambda peer: head_ref.at[peer], head_in, head_sems.at[0], head_sems.at[1])
    head_in[me] = head_ref[me]
    collect(n, head_in, head_sems.at[1])
    head_sum[...] = jnp.sum(head_in[...], 0)
    head_all[me] = head_sum[...]
    spread(n, me, lambda peer: head_sum, head_all, head_sems.at[2], head_sems.at[3])

    def hop(step, _):
        terms(step)
        for i, cut in enumerate(cuts):
            ring_copy(step - 1, i).wait_recv()
            ring_out[step, cut] = (
                own[cut]
                + sib_in[step, cut].astype(jnp.float32)
                + ring_in[step - 1, cut].astype(jnp.float32)
            ).astype(jnp.bfloat16)
            ring_copy(step, i).start()
        return 0

    lax.fori_loop(1, last, hop, 0)
    terms(last)
    for i, cut in enumerate(cuts):
        ring_copy(last - 1, i).wait_recv()
        grad_ref[cut] = (
            own[cut]
            + sib_in[last, cut].astype(jnp.float32)
            + ring_in[last - 1, cut].astype(jnp.float32)
        )
    collect(n, head_all, head_sems.at[3])
    heads_ref[...] = head_all[...]
    collect(n, head_in, head_sems.at[0])
    collect(n, head_all, head_sems.at[2])

    def drain(step, _):
        sib_copy(step).wait_send()

        @pl.when(step < last)
        def _():
            for i in range(len(cuts)):
                ring_copy(step, i).wait_send()

        return 0

    lax.fori_loop(0, r.ring, drain, 0)


def backward(n, normed, ghid, head):
    rows, width = ghid.shape
    shard = normed.shape[1] // n
    blocks = normed.reshape(rows, n, shard).transpose(1, 0, 2)
    count = len(pieces(shard))
    ring = n // 2
    vmem = pl.BlockSpec(memory_space=pltpu.VMEM)
    sems = pltpu.SemaphoreType.DMA
    return pl.pallas_call(
        functools.partial(backward_kernel, n),
        name="backward",
        out_shape=(
            jax.ShapeDtypeStruct((shard, width), jnp.float32),
            jax.ShapeDtypeStruct(head.shape, jnp.float32),
        ),
        in_specs=[vmem, vmem, vmem],
        out_specs=(vmem, vmem),
        scratch_shapes=[
            pltpu.VMEM((shard, width), jnp.float32),
            pltpu.VMEM((ring, shard, width), jnp.bfloat16),
            pltpu.VMEM((ring, shard, width), jnp.bfloat16),
            pltpu.VMEM((ring - 1, shard, width), jnp.bfloat16),
            pltpu.VMEM((ring - 1, shard, width), jnp.bfloat16),
            pltpu.VMEM(head.shape, jnp.float32),
            pltpu.VMEM(head.shape[1:], jnp.float32),
            pltpu.VMEM(head.shape, jnp.float32),
            sems((ring - 1, count)),
            sems((ring - 1, count)),
            sems((ring,)),
            sems((ring,)),
            sems((4,)),
        ],
        compiler_params=pltpu.CompilerParams(
            collective_id=1, has_side_effects=True, vmem_limit_bytes=60 << 20
        ),
        cost_estimate=pl.CostEstimate(
            flops=2 * rows * width * width, bytes_accessed=32 * rows * width, transcendentals=0
        ),
    )(blocks, ghid, head)


def advantages(reward, value_old, done):
    keep = 1.0 - done.astype(jnp.float32)
    deltas = reward + GAMMA * value_old[:, 1:] * keep - value_old[:, :-1]

    def walk(carry, inputs):
        dstep, kstep = inputs
        carry = dstep + GAMMA * LAMBDA_GAE * kstep * carry
        return (carry, carry)

    start = jnp.zeros((reward.shape[0],), jnp.float32)
    _, stacked = lax.scan(walk, start, (deltas.T, keep.T), reverse=True)
    gae = stacked.T
    return (gae.reshape(-1), (gae + value_old[:, :-1]).reshape(-1))


def split3(value):
    first = lax.reduce_precision(value, 8, 7)
    second = lax.reduce_precision(value - first, 8, 7)
    third = value - first - second
    return [part.astype(jnp.bfloat16) for part in (first, second, third)]


def local(
    obs_feat,
    reward,
    value_old,
    done,
    minibatch_perm,
    old_mean,
    noise,
    gain_in,
    out_weight,
    head_weight,
    log_std,
):
    gae, returns = advantages(reward, value_old, done)
    local_rows, width = obs_feat.shape
    devices = lax.axis_size("fsdp")
    total_rows = local_rows * devices
    xf = obs_feat.astype(jnp.float32)
    normed = (xf * lax.rsqrt(jnp.mean(xf * xf, -1, keepdims=True) + NORM_EPS) * gain_in).astype(
        jnp.bfloat16
    )
    lane = lax.broadcasted_iota(jnp.int32, (8, 128), 1)
    stat = jnp.where(lane == 0, jnp.sum(gae), jnp.where(lane == 1, jnp.sum(gae * gae), 0.0))
    hidden, sums = forward(devices, obs_feat, normed, stat, out_weight)

    per_peer = local_rows // devices
    send_slot = minibatch_perm // local_rows * per_peer + minibatch_perm % per_peer
    place = (jnp.arange(local_rows)[:, None] == send_slot[None, :]).astype(jnp.bfloat16)
    send_hidden = jnp.dot(place, hidden.astype(jnp.bfloat16), preferred_element_type=jnp.bfloat16)
    hidden_out = lax.all_to_all(send_hidden, "fsdp", split_axis=0, concat_axis=0, tiled=True)

    mean_adv = sums[0, 0] / total_rows
    var_adv = sums[0, 1] / total_rows - mean_adv * mean_adv
    adv_b = ((gae - mean_adv) * lax.rsqrt(var_adv + NORM_EPS)).astype(jnp.bfloat16)
    ret_b = returns.astype(jnp.bfloat16)
    scale = 1.0 / jnp.sqrt(jnp.float32(total_rows))
    rinv = lax.rsqrt(jnp.mean(hidden * hidden, -1, keepdims=True) + NORM_EPS)
    hnorm = hidden * rinv
    hnorm_b = hnorm.astype(jnp.bfloat16)
    heads = jnp.dot(hnorm_b, head_weight, preferred_element_type=jnp.float32)
    nact = log_std.shape[0]
    mean_act = heads[:, :nact]
    value = heads[:, nact]
    std_dev = jnp.exp(log_std)
    offset = old_mean.astype(jnp.float32) - mean_act
    sample = noise.astype(jnp.float32)
    logr = jnp.sum(-sample * offset / std_dev - offset * offset / (2.0 * std_dev * std_dev), -1)
    ratio = jnp.exp(logr)
    advant = adv_b.astype(jnp.float32)
    clipped = jnp.clip(ratio, 1.0 - CLIP_EPS, 1.0 + CLIP_EPS)
    active = ratio * advant <= clipped * advant
    gratio = jnp.where(active, -scale * advant, 0.0)
    glogr = gratio * ratio
    gmean = glogr[:, None] * (sample / std_dev + offset / (std_dev * std_dev))
    gvalue = scale * (value - ret_b.astype(jnp.float32))
    std_local = jnp.sum(
        glogr[:, None] * (sample * offset / std_dev + offset * offset / (std_dev * std_dev)), 0
    )
    ghead = jnp.concatenate([gmean, gvalue[:, None]], 1)
    parts = split3(ghead)
    head_local = sum(
        lax.dot_general(part, hnorm_b, (((0,), (0,)), ((), ())), preferred_element_type=jnp.float32)
        for part in parts
    )
    ghn = sum(
        lax.dot_general(part, head_weight, (((1,), (1,)), ((), ())), preferred_element_type=jnp.float32)
        for part in parts
    )
    ghid = rinv * (ghn - hnorm * jnp.mean(ghn * hnorm, -1, keepdims=True))
    ghid_b = ghid.astype(jnp.bfloat16)

    share = width // devices
    block = jnp.zeros((devices, 16, share), jnp.float32)
    block = block.at[:, : nact + 1].set(head_local.reshape(nact + 1, devices, share).swapaxes(0, 1))
    block = block.at[:, nact + 1, :nact].set(std_local)
    grad_weight, heads_all = backward(devices, normed, ghid_b, block)
    grad_head = heads_all[:, : nact + 1].swapaxes(0, 1).reshape(nact + 1, width).T
    grad_std = heads_all[0, nact + 1, :nact]
    return (hidden_out, grad_weight, grad_head, grad_std)


def solution(mesh):
    return jax.shard_map(
        local,
        mesh=mesh,
        in_specs=(
            P(("groups", "fsdp"), None),
            P(("groups", "fsdp"), None),
            P(("groups", "fsdp"), None),
            P(("groups", "fsdp"), None),
            P(("groups", "fsdp")),
            P(("groups", "fsdp"), None),
            P(("groups", "fsdp"), None),
            P(),
            P("fsdp", None),
            P(),
            P(),
        ),
        out_specs=(
            P(("groups", "fsdp"), None),
            P(("groups", "fsdp"), None),
            P("groups", None),
            P("groups"),
        ),
        check_vma=False,
    )
```

time: 390 us -> 167 us (0.43)
  waiting for transfers between devices: 247 us -> 0.01 us
  Pallas kernels: 0 us -> 122 us
  blocking collectives: 77.6 us -> 0 us
  matrix products: 26 us -> 11 us
  between operations: 16.5 us -> 3.57 us
  local copies, waits for them, and re-layouts: 3.81 us -> 13.3 us
    reduce_scatter x1 -> x0, waiting for transfers between devices: 183 us -> none  [compute_rows(): lax.psum_scatter(lax.dot_general(columns, ghid_b, (((0,), (0,)), ((), ())...]
    pallas_call x0 -> x2, Pallas kernels: none -> 122 us  [the longest x1 69.3 us: backward(): pl.pallas_call(functools.partial(backward_kernel, n), name='backward', ou...]
    psum x2 -> x0, blocking collectives: 77.6 us -> none  [the longest x1 52.4 us: compute_rows(): grad_head, grad_std = lax.psum((head_local, std_local), 'fsdp')]
    all_gather x1 -> x0, waiting for transfers between devices: 42.8 us -> none  [compute_rows(): lax.all_gather(out_weight, 'fsdp', axis=0, tiled=True)]
    psum x1 -> x0, waiting for transfers between devices: 20.8 us -> none  [compute_rows(): grad_head, grad_std = lax.psum((head_local, std_local), 'fsdp')]
    dot_general x5 -> x8, matrix products: 26 us -> 11 us  [the longest x1 4.19 us: local(): jnp.dot(place, hidden.astype(jnp.bfloat16), preferred_element_type=jnp.bf...]
    scatter x1 -> x0, other arithmetic: 4.11 us -> none  [local(): send_hidden = jnp.zeros_like(hidden_local).at[send_slot].set(hidden_local)]
  transfers between devices with their start and end apart: 4 -> 1, of which waited for: 3 -> 0; matrix products, arithmetic and copies ran while one was open for 6% -> 9% of each run, Pallas kernels for 0% -> 42%
where the time goes in v1:
time: 167 us; the launch traced here: 164 us
  Pallas kernels  122 us (73%)
  local copies, waits for them, and re-layouts  13.3 us (8%)
  matrix products  11 us (7%)
  other arithmetic  9.06 us (5%)
  starting transfers between devices  4.61 us (3%)
  between operations  3.57 us (2%)
    pallas_call x1, Pallas kernels, backward(): pl.pallas_call(functools.partial(backward_kernel, n), name='backward', ou...  69.3 us
    pallas_call x1, Pallas kernels, forward(): pl.pallas_call(functools.partial(forward_kernel, n), name='forward', out_...  52.9 us
    unnamed x30, local copies, waits for them, and re-layouts  6.51 us
    all_to_all x1, starting transfers between devices, local(): lax.all_to_all(send_hidden, 'fsdp', split_axis=0, concat_axis=0, tiled=True)  4.61 us
    dot_general x1, matrix products, local(): jnp.dot(place, hidden.astype(jnp.bfloat16), preferred_element_type=jnp.bf...  4.19 us
  transfers between devices with their start and end apart: 1, of which 0 were waited for; matrix products, arithmetic and copies ran while one was open for 9% of the time, Pallas kernels for 42%

profile of v1, /device:TPU:9, one launch (start us, length us, event | category | flops | bytes accessed | tf_op | source)
XLA Modules:
  0.0 164.1 jit_solution(7542560466267232586)
XLA Ops:
  0.6 0.0 copy-start
  0.6 0.0 copy-start.8
  0.7 0.9 fusion.23
  1.5 0.1 copy.32
  1.6 0.1 copy.33
  1.7 1.8 %while.19 = (s32[]{:T(128)}, f32[16]{0:T(128)S(1)}, f32[24,16]{1,0:T(8,128)S(1)}, f32[24,16]{1,0:T(8,128)S(1)}, f32[24,16]{1,0:T(8,128)S(1)}, /*index=5*/s32[]{:T(128)}, s32[]{:T(128)}, s32[]{:T(128)}) while((s32[]{:T(128)}, f32[16]{0:T(128)S(1)}, f32[24,16]{1,0:T(8,128)S(1)}, f32[24,16]{1,0:T(8,128)S(1)}, f32[24,16]{1,0:T(8,128)S(1)}, ...), condition=%wide.region_2.3_spmd.clone, body=%wide.region_1.2_spmd.clone.sunk | while | flops 68 | bytes 499 | solution.py:346
  3.5 0.1 copy.34
  3.5 0.6 reduce_sum.64
  4.2 0.6 fusion.19
  4.8 0.6 compare_select_fusion
  5.4 1.9 %copy.30 = bf16[384,2048]{0,1:T(8,128)(2,1)S(1)} copy(bf16[384,2048]{1,0:T(8,128)(2,1)} %x_ref.1) | data formatting | bytes 3145728 | tf_op args[0]
  7.3 0.4 fusion.2
  7.7 0.0 copy-start.9
  7.7 0.4 fusion.4
  8.2 1.6 copy.31
  9.8 0.0 copy-done.9
  9.8 1.2 broadcast_select_fusion.1.stat_ref
  11.0 52.9 %forward.1 = (f32[384,2048]{1,0:T(8,128)}, f32[8,128]{1,0:T(8,128)}) custom-call(bf16[384,2048]{1,0:T(8,128)(2,1)} %x_ref.1, bf16[16,384,128]{2,1,0:T(8,128)(2,1)} %bitcast.62, f32[8,128]{1,0:T(8,128)} %broadcast_select_fusion.1.stat_ref, bf16[128,2048]{1,0:T(8,128)(2,1)} %w_ref.1), custom_call_target="tpu_custom_call" | custom-call | flops 3221225472 | bytes 12582912 | tf_op jit(solution)/shard_map/forward/pallas_call | solution.py:173
  63.9 4.2 %fusion.5 = bf16[384,2048]{1,0:T(8,128)(2,1)} fusion(f32[384,2048]{1,0:T(8,128)} %get-tuple-element.136, s32[384]{0:T(512)S(1)} %fusion.26), kind=kOutput, calls=%fused_computation.15 | convolution fusion | flops 604913664 | bytes 4720128 | tf_op jit(solution)/shard_map/dot_general | solution.py:386
  68.1 4.6 %all-to-all-start = ((bf16[16,24,2048]{2,1,0:T(8,128)(2,1)}), bf16[16,24,2048]{2,1,0:T(8,128)(2,1)}, u32[]{:S(2)}, u32[]{:S(2)}) async-start(bf16[16,24,2048]{2,1,0:T(8,128)(2,1)} %bitcast.60), calls=%async_computation | async-start | bytes 3145728 | tf_op jit(solution)/shard_map/all_to_all | solution.py:387
  72.8 0.0 copy-done.1
  72.8 0.3 multiply_reduce_fusion.1
  73.1 1.3 fusion.34
  77.0 0.1 reshape.169
  77.1 0.0 copy-start.6
  77.1 0.0 copy-start.7
  77.1 1.4 multiply_convert_fusion.1
  78.5 0.1 reshape.170
  78.6 2.0 %fusion.36 = f32[384,13]{0,1:T(8,128)S(1)} fusion(bf16[384,2048]{1,0:T(8,128)(2,1)} %multiply_convert_fusion.1, bf16[2048,13]{0,1:T(8,128)(2,1)S(1)} %copy-done), kind=kOutput, calls=%fused_computation.78 | convolution fusion | flops 20447232 | bytes 1646080 | tf_op jit(solution)/shard_map/dot_general | solution.py:397
  80.7 0.0 copy-done.6
  80.7 0.1 fusion.17
  80.8 0.2 fusion.18
  81.0 1.7 %fusion.29 = f32[13,2048]{1,0:T(8,128)S(1)} fusion(bf16[384,2048]{1,0:T(8,128)(2,1)} %multiply_convert_fusion.1, f32[384,1]{0,1:T(1,128)S(1)} %fusion.28, f32[384,12]{0,1:T(8,128)S(1)} %get-tuple-element.174), kind=kOutput, calls=%fused_computation.72 | convolution fusion | flops 20462208 | bytes 1699328 | tf_op jit(solution)/shard_map/dot_general | solution.py:419
  82.8 0.3 convolution_add_fusion.1
  83.1 0.3 convolution_add_fusion
  83.6 0.4 scatter.9.head_ref
  83.9 0.0 copy-start.4
  83.9 0.6 fusion.31
  84.5 0.6 fusion.30
  85.2 1.2 multiply_reduce_fusion
  86.4 1.7 %multiply_convert_fusion.ghid_ref = bf16[384,2048]{1,0:T(8,128)(2,1)} fusion(f32[384,2048]{1,0:T(8,128)S(1)} %get-tuple-element.185, f32[384,2048]{1,0:T(8,128)S(1)} %copy-done.1, f32[384]{0:T(512)S(1)} %broadcast_multiply_fusion, f32[384]{0:T(512)S(1)} %add_rsqrt_fusion), kind=kLoop, calls=%fused_computation.8 | loop fusion | flops 3932160 | bytes 7867392 | tf_op jit(solution)/shard_map/convert_element_type | solution.py:427
  88.1 69.3 %backward.1 = (f32[128,2048]{1,0:T(8,128)}, f32[16,16,128]{2,1,0:T(8,128)}) custom-call(bf16[16,384,128]{2,1,0:T(8,128)(2,1)} %bitcast.63, bf16[384,2048]{1,0:T(8,128)(2,1)} %multiply_convert_fusion.ghid_ref, f32[16,16,128]{2,1,0:T(8,128)} %copy-done.4), custom_call_target="tpu_custom_call" | custom-call | flops 3221225472 | bytes 25165824 | tf_op jit(solution)/shard_map/backward/pallas_call | solution.py:303
  157.4 1.0 slice_bitcast_fusion
  158.5 0.7 copy.38
  159.2 1.2 slice_bitcast_fusion.1
  160.4 0.0 all-to-all-done
  160.4 2.7 %copy.54 = bf16[384,2048]{1,0:T(8,128)(2,1)} copy(bf16[384,2048]{1,0:T(8,128)(2,1)} %bitcast.6) | data formatting | bytes 3145728
  163.1 1.0 copy.55
  (79 shorter events, 1.7 us)
Async XLA Ops:
  0.6 78.0 %copy-start = (bf16[2048,13]{0,1:T(8,128)(2,1)S(1)}, bf16[2048,13]{0,1:T(8,128)(2,1)}, u32[]{:S(2)}) copy-start(bf16[2048,13]{0,1:T(8,128)(2,1)} %param.26) | copy-start | bytes 159748
  0.6 7.1 %copy-start.8 = (f32[2048]{0:T(1024)S(1)}, f32[2048]{0:T(1024)}, u32[]{:S(2)}) copy-start(f32[2048]{0:T(1024)} %param.24) | copy-start | bytes 24580
  7.7 2.1 %copy-start.9 = (s32[384]{0:T(512)S(1)}, s32[384]{0:T(512)}, u32[]{:S(2)}) copy-start(s32[384]{0:T(512)} %param.21) | copy-start | bytes 4612
  63.9 8.8 %copy-start.1 = (f32[384,2048]{1,0:T(8,128)S(1)}, f32[384,2048]{1,0:T(8,128)}, u32[]{:S(2)}) copy-start(f32[384,2048]{1,0:T(8,128)} %get-tuple-element.136) | copy-start | bytes 9437188
  68.1 8.9 %copy-start.5 = (f32[16,25]{1,0:T(8,128)S(1)}, f32[16,25]{1,0:T(8,128)}, u32[]{:S(2)}) copy-start(f32[16,25]{1,0:T(8,128)} %param.19) | copy-start | bytes 4804
  68.1 92.3 %all-to-all-start = ((bf16[16,24,2048]{2,1,0:T(8,128)(2,1)}), bf16[16,24,2048]{2,1,0:T(8,128)(2,1)}, u32[]{:S(2)}, u32[]{:S(2)}) async-start(bf16[16,24,2048]{2,1,0:T(8,128)(2,1)} %bitcast.60), calls=%async_computation | async-start | bytes 3145728 | tf_op jit(solution)/shard_map/all_to_all | solution.py:387
  73.0 5.5 %copy-start.10 = (f32[12]{0:T(128)S(1)}, f32[12]{0:T(128)}, u32[]{:S(2)}) copy-start(f32[12]{0:T(128)} %param.27) | copy-start | bytes 148
  77.1 3.6 %copy-start.6 = (bf16[384,12]{0,1:T(8,128)(2,1)S(1)}, bf16[384,12]{0,1:T(8,128)(2,1)}, u32[]{:S(2)}) copy-start(bf16[384,12]{0,1:T(8,128)(2,1)} %param.23) | copy-start | bytes 27652
  77.1 3.6 %copy-start.7 = (bf16[384,12]{0,1:T(8,128)(2,1)S(1)}, bf16[384,12]{0,1:T(8,128)(2,1)}, u32[]{:S(2)}) copy-start(bf16[384,12]{0,1:T(8,128)(2,1)} %param.22) | copy-start | bytes 27652
  78.6 4.1 %copy-start.2 = (bf16[384,2048]{1,0:T(8,128)(2,1)S(1)}, bf16[384,2048]{1,0:T(8,128)(2,1)}, u32[]{:S(2)}) copy-start(bf16[384,2048]{1,0:T(8,128)(2,1)} %multiply_convert_fusion.1) | copy-start | bytes 4718596
  83.9 1.2 copy-start.4
  157.4 5.7 %copy-start.3 = (f32[128,2048]{1,0:T(8,128)S(1)}, f32[128,2048]{1,0:T(8,128)}, u32[]{:S(2)}) copy-start(f32[128,2048]{1,0:T(8,128)} %get-tuple-element.246) | copy-start | bytes 3145732

commit v2 on v1

v2 whole, which is shorter than its diff:
```python
import functools

import jax
import jax.numpy as jnp
from jax import lax
from jax.experimental import pallas as pl
from jax.experimental.pallas import tpu as pltpu
from jax.sharding import PartitionSpec as P

GAMMA = 0.99
LAMBDA_GAE = 0.95
CLIP_EPS = 0.2
NORM_EPS = 1e-05
MESH = pl.DeviceIdType.MESH
TILE = 512
STRIP = 128


def chip_at(pos, ring):
    half = ring // 2
    col = pos // half
    row = col * (ring - 1 - pos) + (1 - col) * pos
    return 2 * row + col


class Ring:
    def __init__(self, n):
        self.n = n
        self.me = lax.axis_index("fsdp")
        self.ring = n // 2
        self.core = lax.rem(self.me, 2)
        chip = self.me // 2
        col = lax.rem(chip, 2)
        row = chip // 2
        self.pos = col * (self.ring - 1 - row) + (1 - col) * row
        self.step = 1 - 2 * self.core
        self.sibling = self.me + self.step

    def device(self, ahead, core):
        pos = lax.rem(self.pos + ahead + self.ring, self.ring)
        return 2 * chip_at(pos, self.ring) + core

    def down(self):
        return self.device(self.step, self.core)


def enter(n, me):
    barrier = pltpu.get_barrier_semaphore()

    @pl.loop(1, n)
    def _(k):
        pl.semaphore_signal(
            barrier, inc=1, device_id={"fsdp": lax.rem(me + k, n)}, device_id_type=MESH
        )

    pl.semaphore_wait(barrier, n - 1)


def remote(src, dst, send, recv, device):
    return pltpu.make_async_remote_copy(
        src_ref=src,
        dst_ref=dst,
        send_sem=send,
        recv_sem=recv,
        device_id={"fsdp": device},
        device_id_type=MESH,
    )


def pieces(rows):
    count = 2 if rows % 32 == 0 else 1
    return [pl.ds(i * (rows // count), rows // count) for i in range(count)]


def spread(n, me, source_of, dst, send, recv):
    @pl.loop(1, n)
    def _(k):
        peer = lax.rem(me + k, n)
        remote(source_of(peer), dst.at[me], send, recv, peer).start()


def collect(n, slots, sem):
    part = slots.at[pl.ds(0, n - 1)]
    pltpu.make_async_copy(part, part, sem).wait()


def step_kernel(
    n, nact, per, burst, aligned,
    x_ref, lhs_ref, w_ref, gain_ref, gae_ref, ret_ref, slot_ref, mean_ref, noise_ref, head_ref, std_ref,
    out_ref, grad_ref, heads_ref,
    normed, held, hidden, hidden_b, hnorm_b, rinv, ghid, ghead, ghead3, ordered,
    stat, stats, own, sib_out, sib_in, ring_out, ring_in, head_out, head_in, head_sum, head_all,
    local_sem, gat_send, gat_recv, gsib_send, gsib_recv,
    ring_send, ring_recv, sib_send, sib_recv, small_sems,
):
    r = Ring(n)
    me, last = r.me, r.ring - 1
    rows, width = x_ref.shape
    shard = w_ref.shape[0]
    first = pltpu.make_async_copy(w_ref, held.at[me], local_sem.at[0])
    first.start()
    gae = gae_ref[...]
    lane = lax.broadcasted_iota(jnp.int32, stat.shape, 1)
    stat[...] = jnp.where(
        lane == 0,
        jnp.sum(gae, axis=1, keepdims=True),
        jnp.where(lane == 1, jnp.sum(gae * gae, axis=1, keepdims=True), 0.0),
    )
    enter(n, me)
    cuts = pieces(shard)
    down = r.down()

    def gather_copy(owner, step, i):
        part = held.at[owner, cuts[i]]
        return remote(part, part, gat_send.at[step, i], gat_recv.at[step, i], down)

    def gather_sib(owner, step, i):
        part = held.at[owner, cuts[i]]
        return remote(part, part, gsib_send.at[step, i], gsib_recv.at[step, i], r.sibling)

    def mine(step):
        return r.device(-r.step * step, r.core)

    def theirs(step):
        return r.device(r.step * step, 1 - r.core)

    def columns(owner):
        if not aligned:
            return lhs_ref[owner]
        return normed[:, pl.ds(pl.multiple_of(owner * shard, shard), shard)]

    def add(owner):
        left = columns(owner)
        for j in range(0, width, TILE):
            cols = pl.ds(j, TILE)
            hidden[:, cols] += jnp.dot(
                left, held[owner, :, cols], preferred_element_type=jnp.float32
            )

    first.wait()
    for i in range(len(cuts)):
        gather_copy(me, 1, i).start()
        gather_sib(me, 0, i).start()
    spread(n, me, lambda peer: stat, stats, small_sems.at[4], small_sems.at[5])
    stats[me] = stat[...]

    @pl.loop(0, rows // STRIP)
    def _(t):
        strip = pl.ds(pl.multiple_of(t * STRIP, STRIP), STRIP)
        xf = x_ref[strip].astype(jnp.float32)
        hidden[strip] = xf
        if aligned:
            scale = lax.rsqrt(jnp.mean(xf * xf, -1, keepdims=True) + NORM_EPS)
            normed[strip] = (xf * scale * gain_ref[...]).astype(jnp.bfloat16)

    def gather_hop(step, _):
        owner = mine(step)
        for i in range(len(cuts)):
            gather_copy(owner, step, i).wait_recv()

            @pl.when(step < last)
            def _():
                gather_copy(owner, step + 1, i).start()

            gather_sib(owner, step, i).start()
            if i == 0:
                add(mine(step - 1))
        for i in range(len(cuts)):
            gather_sib(theirs(step - 1), step - 1, i).wait_recv()
        add(theirs(step - 1))
        return 0

    lax.fori_loop(1, r.ring, gather_hop, 0)
    add(mine(last))
    for i in range(len(cuts)):
        gather_sib(theirs(last), last, i).wait_recv()
    add(theirs(last))

    @pl.loop(0, rows // STRIP)
    def _(t):
        strip = pl.ds(pl.multiple_of(t * STRIP, STRIP), STRIP)
        h = hidden[strip]
        hidden_b[strip] = h.astype(jnp.bfloat16)
        scale = lax.rsqrt(jnp.mean(h * h, -1, keepdims=True) + NORM_EPS)
        rinv[strip] = scale
        hnorm_b[strip] = (h * scale).astype(jnp.bfloat16)

    slots = n * per
    place = (
        lax.broadcasted_iota(jnp.int32, (slots, rows), 0)
        == jnp.broadcast_to(slot_ref[...], (slots, rows))
    ).astype(jnp.float32).astype(jnp.bfloat16)
    for j in range(0, width, TILE):
        cols = pl.ds(j, TILE)
        moved = jnp.dot(place, hidden_b[:, cols], preferred_element_type=jnp.float32)
        ordered[:, :, cols] = moved.reshape(n, per, TILE).astype(jnp.bfloat16)

    def row_copy(peer):
        return remote(ordered.at[peer], out_ref.at[me], small_sems.at[6], small_sems.at[7], peer)

    @pl.loop(1, burst)
    def _(k):
        row_copy(lax.rem(me + k, n)).start()

    def more_rows(step):
        for u in range(2):
            k = burst + 2 * step + u

            @pl.when(k < n)
            def _():
                row_copy(lax.rem(me + k, n)).start()

    kept = pltpu.make_async_copy(ordered.at[me], out_ref.at[me], local_sem.at[1])
    kept.start()

    collect(n, stats, small_sems.at[5])
    sums = jnp.sum(stats[...], 0)
    total_rows = rows * n
    mean_adv = sums[0:1, 0:1] / total_rows
    var_adv = sums[0:1, 1:2] / total_rows - mean_adv * mean_adv
    advant = ((gae - mean_adv) * lax.rsqrt(var_adv + NORM_EPS)).astype(jnp.bfloat16).astype(jnp.float32)
    returns = ret_ref[...].astype(jnp.bfloat16).astype(jnp.float32)
    scale = 1.0 / jnp.sqrt(jnp.full((1, 1), total_rows, jnp.float32))
    heads = lax.dot_general(
        head_ref[0:16], hnorm_b[...], (((1,), (1,)), ((), ())), preferred_element_type=jnp.float32
    )
    std_dev = jnp.exp(std_ref[...])
    offset = mean_ref[...].astype(jnp.float32) - heads[0:nact]
    sample = noise_ref[...].astype(jnp.float32)
    logr = jnp.sum(
        -sample * offset / std_dev - offset * offset / (2.0 * std_dev * std_dev), 0, keepdims=True
    )
    ratio = jnp.exp(logr)
    clipped = jnp.clip(ratio, 1.0 - CLIP_EPS, 1.0 + CLIP_EPS)
    gratio = jnp.where(ratio * advant <= clipped * advant, -scale * advant, 0.0)
    glogr = gratio * ratio
    ghead[...] = jnp.zeros_like(ghead)
    ghead[0:nact] = glogr * (sample / std_dev + offset / (std_dev * std_dev))
    ghead[nact : nact + 1] = scale * (heads[nact : nact + 1] - returns)
    std_local = jnp.sum(
        glogr * (sample * offset / std_dev + offset * offset / (std_dev * std_dev)), 1, keepdims=True
    )
    rest = ghead[...]
    for k in range(3):
        term = rest.astype(jnp.bfloat16)
        ghead3[16 * k : 16 * k + 16] = term
        rest = rest - term.astype(jnp.float32)

    @pl.loop(0, rows // STRIP)
    def _(t):
        strip = pl.ds(pl.multiple_of(t * STRIP, STRIP), STRIP)
        ghn = lax.dot_general(
            ghead3[:, strip], head_ref[...], (((0,), (0,)), ((), ())),
            preferred_element_type=jnp.float32,
        )
        hnorm = hidden[strip] * rinv[strip]
        inner = jnp.mean(ghn * hnorm, -1, keepdims=True)
        ghid[strip] = (rinv[strip] * (ghn - hnorm * inner)).astype(jnp.bfloat16)

    def product(owner, cols):
        return lax.dot_general(
            columns(owner), ghid[:, cols], (((0,), (0,)), ((), ())),
            preferred_element_type=jnp.float32,
        )

    def ring_copy(step, i):
        return remote(
            ring_out.at[step, cuts[i]], ring_in.at[step, cuts[i]],
            ring_send.at[step, i], ring_recv.at[step, i], down,
        )

    def sib_copy(step):
        return remote(
            sib_out.at[step], sib_in.at[step], sib_send.at[step], sib_recv.at[step], r.sibling
        )

    def terms(step):
        other = r.device(-r.step * (last - step), 1 - r.core)
        for j in range(0, width, TILE):
            cols = pl.ds(j, TILE)
            sib_out[step, :, cols] = product(other, cols).astype(jnp.bfloat16)
        sib_copy(step).start()
        target = r.device(r.step * (last - step), r.core)
        for j in range(0, width, TILE):
            cols = pl.ds(j, TILE)
            own[:, cols] = product(target, cols)
        sib_copy(step).wait_recv()

    terms(0)
    for i, cut in enumerate(cuts):
        ring_out[0, cut] = (own[cut] + sib_in[0, cut].astype(jnp.float32)).astype(jnp.bfloat16)
        ring_copy(0, i).start()
    more_rows(0)

    head_local = jnp.dot(ghead3[...], hnorm_b[...], preferred_element_type=jnp.float32)
    head_local = head_local[0:16] + head_local[16:32] + head_local[32:48]
    share = width // n
    diagonal = lax.broadcasted_iota(jnp.int32, (nact, share), 0) == lax.broadcasted_iota(
        jnp.int32, (nact, share), 1
    )
    std_row = jnp.sum(jnp.where(diagonal, std_local, 0.0), 0, keepdims=True)
    line = lax.broadcasted_iota(jnp.int32, (16, share), 0)
    for j in range(n):
        head_out[j] = jnp.where(
            line == nact + 1, std_row, head_local[:, j * share : (j + 1) * share]
        )
    spread(n, me, lambda peer: head_out.at[peer], head_in, small_sems.at[0], small_sems.at[1])
    head_in[me] = head_out[me]

    def hop(step, _):
        terms(step)
        for i, cut in enumerate(cuts):
            ring_copy(step - 1, i).wait_recv()
            ring_out[step, cut] = (
                own[cut]
                + sib_in[step, cut].astype(jnp.float32)
                + ring_in[step - 1, cut].astype(jnp.float32)
            ).astype(jnp.bfloat16)
            ring_copy(step, i).start()
        more_rows(step)
        return 0

    lax.fori_loop(1, r.ring // 2, hop, 0)
    collect(n, head_in, small_sems.at[1])
    head_sum[...] = jnp.sum(head_in[...], 0)
    head_all[me] = head_sum[...]
    spread(n, me, lambda peer: head_sum, head_all, small_sems.at[2], small_sems.at[3])
    lax.fori_loop(r.ring // 2, last, hop, 0)
    terms(last)
    more_rows(last)
    for i, cut in enumerate(cuts):
        ring_copy(last - 1, i).wait_recv()
        grad_ref[cut] = (
            own[cut]
            + sib_in[last, cut].astype(jnp.float32)
            + ring_in[last - 1, cut].astype(jnp.float32)
        )
    collect(n, head_all, small_sems.at[3])
    heads_ref[...] = head_all[...]
    kept.wait()
    collect(n, out_ref, small_sems.at[7])
    collect(n, ordered, small_sems.at[6])
    collect(n, stats, small_sems.at[4])
    collect(n, head_in, small_sems.at[0])
    collect(n, head_all, small_sems.at[2])

    def drain(step, _):
        owner = mine(step)
        for i in range(len(cuts)):
            @pl.when(step < last)
            def _():
                gather_copy(owner, step + 1, i).wait_send()
                ring_copy(step, i).wait_send()

            gather_sib(owner, step, i).wait_send()
        sib_copy(step).wait_send()
        return 0

    lax.fori_loop(0, r.ring, drain, 0)


def step_call(n, x, weight, gain, gae, ret, slot, old_mean, noise, head, log_std):
    rows, width = x.shape
    shard = weight.shape[0]
    nact = log_std.shape[0]
    per = -(-(rows // n) // 8) * 8
    aligned = shard % 128 == 0
    blocks = jnp.zeros((8, 128), jnp.bfloat16)
    if not aligned:
        xf = x.astype(jnp.float32)
        normed = xf * lax.rsqrt(jnp.mean(xf * xf, -1, keepdims=True) + NORM_EPS) * gain
        blocks = normed.astype(jnp.bfloat16).reshape(rows, n, shard).transpose(1, 0, 2)
    count = len(pieces(shard))
    ring = n // 2
    share = width // n
    vmem = pl.BlockSpec(memory_space=pltpu.VMEM)
    anywhere = pl.BlockSpec(memory_space=pl.ANY)
    sems = pltpu.SemaphoreType.DMA
    bf16, f32 = jnp.bfloat16, jnp.float32
    return pl.pallas_call(
        functools.partial(step_kernel, n, nact, per, max(n // 4, 1), aligned),
        name="step",
        out_shape=(
            jax.ShapeDtypeStruct((n, per, width), bf16),
            jax.ShapeDtypeStruct((shard, width), f32),
            jax.ShapeDtypeStruct((n, 16, share), f32),
        ),
        in_specs=[vmem, vmem, anywhere] + [vmem] * 8,
        out_specs=(anywhere, vmem, vmem),
        scratch_shapes=[
            pltpu.VMEM((rows, width) if aligned else (16, 128), bf16),
            pltpu.VMEM((n, shard, width), bf16),
            pltpu.VMEM((rows, width), f32),
            pltpu.VMEM((rows, width), bf16),
            pltpu.VMEM((rows, width), bf16),
            pltpu.VMEM((rows, 1), f32),
            pltpu.VMEM((rows, width), bf16),
            pltpu.VMEM((16, rows), f32),
            pltpu.VMEM((48, rows), bf16),
            pltpu.VMEM((n, per, width), bf16),
            pltpu.VMEM((8, 128), f32),
            pltpu.VMEM((n, 8, 128), f32),
            pltpu.VMEM((shard, width), f32),
            pltpu.VMEM((ring, shard, width), bf16),
            pltpu.VMEM((ring, shard, width), bf16),
            pltpu.VMEM((ring - 1, shard, width), bf16),
            pltpu.VMEM((ring - 1, shard, width), bf16),
            pltpu.VMEM((n, 16, share), f32),
            pltpu.VMEM((n, 16, share), f32),
            pltpu.VMEM((16, share), f32),
            pltpu.VMEM((n, 16, share), f32),
            sems((2,)),
            sems((ring, count)),
            sems((ring, count)),
            sems((ring, count)),
            sems((ring, count)),
            sems((ring - 1, count)),
            sems((ring - 1, count)),
            sems((ring,)),
            sems((ring,)),
            sems((8,)),
        ],
        compiler_params=pltpu.CompilerParams(
            collective_id=0, has_side_effects=True, vmem_limit_bytes=66_000_000
        ),
        cost_estimate=pl.CostEstimate(
            flops=4 * rows * width * width, bytes_accessed=32 * rows * width, transcendentals=0
        ),
    )(x, blocks, weight, gain[None], gae, ret, slot, old_mean, noise, head, log_std[:, None])


def advantages(reward, value_old, done):
    keep = 1.0 - done.astype(jnp.float32)
    deltas = reward + GAMMA * value_old[:, 1:] * keep - value_old[:, :-1]

    carry = jnp.zeros((reward.shape[0],), jnp.float32)
    column = []
    for t in reversed(range(reward.shape[1])):
        carry = deltas[:, t] + GAMMA * LAMBDA_GAE * keep[:, t] * carry
        column.append(carry)
    gae = jnp.stack(column[::-1], 1)
    return (gae.reshape(-1), (gae + value_old[:, :-1]).reshape(-1))


def local(
    obs_feat,
    reward,
    value_old,
    done,
    minibatch_perm,
    old_mean,
    noise,
    gain_in,
    out_weight,
    head_weight,
    log_std,
):
    gae, returns = advantages(reward, value_old, done)
    local_rows, width = obs_feat.shape
    devices = lax.axis_size("fsdp")
    nact = log_std.shape[0]
    per_peer = local_rows // devices
    padded = -(-per_peer // 8) * 8
    slot = minibatch_perm // local_rows * padded + minibatch_perm % per_peer
    head = jnp.pad(head_weight.T, ((0, 16 - head_weight.shape[1]), (0, 0)))
    moved, grad_weight, heads_all = step_call(
        devices, obs_feat, out_weight, gain_in, gae[None], returns[None], slot[None],
        old_mean.T, noise.T, jnp.tile(head, (3, 1)), log_std,
    )
    hidden_out = moved[:, :per_peer].reshape(local_rows, width)
    grad_head = heads_all[:, : nact + 1].swapaxes(0, 1).reshape(nact + 1, width).T
    grad_std = heads_all[0, nact + 1, :nact]
    return (hidden_out, grad_weight, grad_head, grad_std)


def solution(mesh):
    return jax.shard_map(
        local,
        mesh=mesh,
        in_specs=(
            P(("groups", "fsdp"), None),
            P(("groups", "fsdp"), None),
            P(("groups", "fsdp"), None),
            P(("groups", "fsdp"), None),
            P(("groups", "fsdp")),
            P(("groups", "fsdp"), None),
            P(("groups", "fsdp"), None),
            P(),
            P("fsdp", None),
            P(),
            P(),
        ),
        out_specs=(
            P(("groups", "fsdp"), None),
            P(("groups", "fsdp"), None),
            P("groups", None),
            P("groups"),
        ),
        check_vma=False,
    )
```

time: 167 us -> 153 us (0.916); the launches traced: 164 us -> 153 us
  Pallas kernels: 122 us -> 138 us
  matrix products: 11 us -> 0 us
  other arithmetic: 9.06 us -> 2.41 us
  starting transfers between devices: 4.61 us -> 0 us
  between operations: 3.57 us -> 0.67 us
    pallas_call x2 -> x1, Pallas kernels: 122 us -> 138 us  [step_call(): pl.pallas_call(functools.partial(step_kernel, n, nact, per, max(n // 4, 1...]
    dot_general x8 -> x0, matrix products: 11 us -> none  [the longest x1 4.19 us: local(): jnp.dot(place, hidden.astype(jnp.bfloat16), preferred_element_type=jnp.bf...]
    all_to_all x1 -> x0, starting transfers between devices: 4.61 us -> none  [local(): lax.all_to_all(send_hidden, 'fsdp', split_axis=0, concat_axis=0, tiled=True)]
    convert_element_type x4 -> x0, other arithmetic: 3.56 us -> none  [the longest x1 1.75 us: local(): ghid_b = ghid.astype(jnp.bfloat16)]
    broadcast_in_dim x1 -> x3, local copies, waits for them, and re-layouts: 0.01 us -> 2.45 us  [the longest x1 1.33 us: step_call(): log_std[:, None]]
    reduce_sum x6 -> x0, other arithmetic: 2.2 us -> none  [the longest x1 0.61 us: local(): jnp.sum(gae)]
    another operation x1 -> x4, local copies, waits for them, and re-layouts: 0.01 us -> 2.16 us  [the longest x1 0.69 us: local(): jnp.tile(head, (3, 1))]
    unnamed x30 -> x6, local copies, waits for them, and re-layouts: 6.51 us -> 4.5 us
  transfers between devices with their start and end apart: 1 -> 0, of which waited for: 0 -> 0; matrix products, arithmetic and copies ran while one was open for 9% -> 0% of each run, Pallas kernels for 42% -> 0%
where the time goes in v2:
time: 153 us
  Pallas kernels  138 us (90%)
  local copies, waits for them, and re-layouts  12.1 us (8%)
  other arithmetic  2.41 us (2%)
    pallas_call x1, Pallas kernels, step_call(): pl.pallas_call(functools.partial(step_kernel, n, nact, per, max(n // 4, 1...  138 us
    unnamed x6, local copies, waits for them, and re-layouts  4.5 us

profile of v2, /device:TPU:9, one launch (start us, length us, event | category | flops | bytes accessed | tf_op | source)
XLA Modules:
  0.0 153.1 jit_solution(10869580041019478162)
XLA Ops:
  0.6 0.7 fusion.47
  1.3 0.5 broadcast_in_dim.14.slot_ref
  1.9 1.3 copy.16.std_ref
  3.2 0.8 add_subtract_fusion
  4.1 0.9 pad.4
  4.9 0.7 tile.4
  5.6 0.2 fusion.46
  5.8 0.1 stack.2
  5.9 0.7 broadcast_in_dim_reshape.6.gae_ref
  6.6 0.7 slice_add_fusion
  7.3 0.7 broadcast_in_dim_reshape.7.ret_ref
  7.9 0.6 broadcast_in_dim.12.lhs_ref
  8.5 137.9 %step.1 = (bf16[16,24,2048]{2,1,0:T(8,128)(2,1)}, f32[128,2048]{1,0:T(8,128)}, f32[16,16,128]{2,1,0:T(8,128)}) custom-call(bf16[384,2048]{1,0:T(8,128)(2,1)} %x_ref.1, bf16[8,128]{1,0:T(8,128)(2,1)} %broadcast_in_dim.12.lhs_ref, bf16[128,2048]{1,0:T(8,128)(2,1)} %w_ref.1, f32[1,2048]{1,0:T(1,128)} %bitcast.24, f32[1,384]{1,0:T(1,128)} %broadcast_in_dim_reshape.6.gae_ref, ...), custom_call_target="tpu_custom_call" | custom-call | flops 6442450944 | bytes 25165824 | tf_op jit(solution)/shard_map/step/pallas_call | solution.py:380
  146.4 1.2 slice_bitcast_fusion.1
  147.6 0.9 slice_bitcast_fusion
  148.6 0.7 copy.18
  149.3 0.0 copy-start
  149.3 2.8 %copy.21 = bf16[384,2048]{1,0:T(8,128)(2,1)} copy(bf16[384,2048]{1,0:T(8,128)(2,1)} %bitcast.16) | data formatting | bytes 3145728
  152.1 0.0 copy-done
  152.1 1.0 copy.22
  (2 shorter events, 0.0 us)
Async XLA Ops:
  149.3 2.8 %copy-start = (f32[128,2048]{1,0:T(8,128)S(1)}, f32[128,2048]{1,0:T(8,128)}, u32[]{:S(2)}) copy-start(f32[128,2048]{1,0:T(8,128)} %get-tuple-element.41) | copy-start | bytes 3145732

commit v3 on v2

--- a/solution.py
+++ b/solution.py
@@ -44,8 +44,10 @@
         return self.device(self.step, self.core)
 
 
-def enter(n, me):
+def enter(n, me, twin):
     barrier = pltpu.get_barrier_semaphore()
+    if twin is not None:
+        pl.semaphore_signal(barrier, inc=1, device_id=twin, device_id_type=MESH)
 
     @pl.loop(1, n)
     def _(k):
@@ -53,7 +55,7 @@
             barrier, inc=1, device_id={"fsdp": lax.rem(me + k, n)}, device_id_type=MESH
         )
 
-    pl.semaphore_wait(barrier, n - 1)
+    pl.semaphore_wait(barrier, n - 1 + (twin is not None))
 
 
 def remote(src, dst, send, recv, device):
@@ -62,7 +64,7 @@
         dst_ref=dst,
         send_sem=send,
         recv_sem=recv,
-        device_id={"fsdp": device},
+        device_id=device if isinstance(device, dict) else {"fsdp": device},
         device_id_type=MESH,
     )
 
@@ -85,38 +87,67 @@
 
 
 def step_kernel(
-    n, nact, per, burst, aligned,
-    x_ref, lhs_ref, w_ref, gain_ref, gae_ref, ret_ref, slot_ref, mean_ref, noise_ref, head_ref, std_ref,
+    n, nact, per, burst, aligned, twinned,
+    x_ref, w_ref, gain_ref, adv_ref, slot_ref, mean_ref, noise_ref, weight_ref, std_ref, lhs_ref,
     out_ref, grad_ref, heads_ref,
     normed, held, hidden, hidden_b, hnorm_b, rinv, ghid, ghead, ghead3, ordered,
     stat, stats, own, sib_out, sib_in, ring_out, ring_in, head_out, head_in, head_sum, head_all,
-    local_sem, gat_send, gat_recv, gsib_send, gsib_recv,
+    local_sem, gat_send, gat_recv, gsib_send, gsib_recv, twin_send, twin_recv, head_ref,
     ring_send, ring_recv, sib_send, sib_recv, small_sems,
 ):
     r = Ring(n)
     me, last = r.me, r.ring - 1
     rows, width = x_ref.shape
     shard = w_ref.shape[0]
-    first = pltpu.make_async_copy(w_ref, held.at[me], local_sem.at[0])
+    first = pltpu.make_async_copy(w_ref, held.at[0, pl.ds(0, shard)], local_sem.at[0])
     first.start()
-    gae = gae_ref[...]
+    gae = adv_ref[0:1]
     lane = lax.broadcasted_iota(jnp.int32, stat.shape, 1)
     stat[...] = jnp.where(
         lane == 0,
         jnp.sum(gae, axis=1, keepdims=True),
         jnp.where(lane == 1, jnp.sum(gae * gae, axis=1, keepdims=True), 0.0),
     )
-    enter(n, me)
+    twin = None
+    group = lax.axis_index("groups")
+    if twinned:
+        twin = {"groups": 1 - group, "fsdp": me}
+    enter(n, me, twin)
     cuts = pieces(shard)
     down = r.down()
 
-    def gather_copy(owner, step, i):
-        part = held.at[owner, cuts[i]]
-        return remote(part, part, gat_send.at[step, i], gat_recv.at[step, i], down)
-
-    def gather_sib(owner, step, i):
-        part = held.at[owner, cuts[i]]
-        return remote(part, part, gsib_send.at[step, i], gsib_recv.at[step, i], r.sibling)
+    if twinned:
+        half, quarter = shard // 2, shard // 4
+        mid = pl.multiple_of(half + quarter * group, quarter)
+        far = pl.multiple_of(half + quarter * (1 - group), quarter)
+        spans = [(0, half), (mid, quarter), (far, quarter)]
+    else:
+        spans = [(0, shard)]
+    rung = spans[:2]
+
+    def gather_copy(step, i):
+        start, size = spans[i]
+        return remote(
+            held.at[step - 1, pl.ds(start, size)], held.at[step, pl.ds(start, size)],
+            gat_send.at[step, i], gat_recv.at[step, i], down,
+        )
+
+    def gather_sib(step, i):
+        start, size = spans[i]
+        return remote(
+            held.at[step, pl.ds(start, size)], held.at[step, pl.ds(shard + start, size)],
+            gsib_send.at[step, i], gsib_recv.at[step, i], r.sibling,
+        )
+
+    def gather_twin(step):
+        part = held.at[step, pl.ds(*spans[1])]
+        return remote(part, part, twin_send.at[step], twin_recv.at[step], twin)
+
+    def from_twin(step):
+        start, size = spans[2]
+        part = held.at[step, pl.ds(start, size)]
+        remote(part, part, twin_send.at[step], twin_recv.at[step], twin).wait_recv()
+        gather_sib(step, 2).start()
 
     def mine(step):
         return r.device(-r.step * step, r.core)
@@ -129,18 +160,31 @@
             return lhs_ref[owner]
         return normed[:, pl.ds(pl.multiple_of(owner * shard, shard), shard)]
 
-    def add(owner):
-        left = columns(owner)
+    def add(step):
+        for i in range(len(spans)):
+            gather_sib(step, i).wait_recv()
+        left = [columns(mine(step)), columns(theirs(step))]
+        if aligned:
+            left = [jnp.concatenate(left, 1)]
+        deep = 2 * shard // len(left)
         for j in range(0, width, TILE):
             cols = pl.ds(j, TILE)
-            hidden[:, cols] += jnp.dot(
-                left, held[owner, :, cols], preferred_element_type=jnp.float32
+            hidden[:, cols] += sum(
+                jnp.dot(
+                    left[k], held[step, k * deep : (k + 1) * deep, cols],
+                    preferred_element_type=jnp.float32,
+                )
+                for k in range(len(left))
             )
 
     first.wait()
-    for i in range(len(cuts)):
-        gather_copy(me, 1, i).start()
-        gather_sib(me, 0, i).start()
+    for i in range(len(spans)):
+        if i < len(rung):
+            gather_copy(1, i).start()
+        gather_sib(0, i).start()
+    head_ref[...] = jnp.zeros_like(head_ref)
+    for k in range(3):
+        head_ref[16 * k : 16 * k + nact + 1] = weight_ref[...]
     spread(n, me, lambda peer: stat, stats, small_sems.at[4], small_sems.at[5])
     stats[me] = stat[...]
 
@@ -154,27 +198,27 @@
             normed[strip] = (xf * scale * gain_ref[...]).astype(jnp.bfloat16)
 
     def gather_hop(step, _):
-        owner = mine(step)
-        for i in range(len(cuts)):
-            gather_copy(owner, step, i).wait_recv()
+        for i in range(len(rung)):
+            gather_copy(step, i).wait_recv()
 
             @pl.when(step < last)
             def _():
-                gather_copy(owner, step + 1, i).start()
-
-            gather_sib(owner, step, i).start()
-            if i == 0:
-                add(mine(step - 1))
-        for i in range(len(cuts)):
-            gather_sib(theirs(step - 1), step - 1, i).wait_recv()
-        add(theirs(step - 1))
+                gather_copy(step + 1, i).start()
+
+            gather_sib(step, i).start()
+            if i == 1:
+                gather_twin(step).start()
+            elif twinned:
+                @pl.when(step > 1)
+                def _():
+                    from_twin(step - 1)
+        add(step - 1)
         return 0
 
     lax.fori_loop(1, r.ring, gather_hop, 0)
-    add(mine(last))
-    for i in range(len(cuts)):
-        gather_sib(theirs(last), last, i).wait_recv()
-    add(theirs(last))
+    if twinned:
+        from_twin(last)
+    add(last)
 
     @pl.loop(0, rows // STRIP)
     def _(t):
@@ -219,12 +263,16 @@
     mean_adv = sums[0:1, 0:1] / total_rows
     var_adv = sums[0:1, 1:2] / total_rows - mean_adv * mean_adv
     advant = ((gae - mean_adv) * lax.rsqrt(var_adv + NORM_EPS)).astype(jnp.bfloat16).astype(jnp.float32)
-    returns = ret_ref[...].astype(jnp.bfloat16).astype(jnp.float32)
+    returns = adv_ref[1:2].astype(jnp.bfloat16).astype(jnp.float32)
     scale = 1.0 / jnp.sqrt(jnp.full((1, 1), total_rows, jnp.float32))
     heads = lax.dot_general(
         head_ref[0:16], hnorm_b[...], (((1,), (1,)), ((), ())), preferred_element_type=jnp.float32
     )
-    std_dev = jnp.exp(std_ref[...])
+    square = (nact, nact)
+    diagonal = lax.broadcasted_iota(jnp.int32, square, 0) == lax.broadcasted_iota(jnp.int32, square, 1)
+    std_dev = jnp.exp(
+        jnp.sum(jnp.where(diagonal, jnp.broadcast_to(std_ref[...], square), 0.0), 1, keepdims=True)
+    )
     offset = mean_ref[...].astype(jnp.float32) - heads[0:nact]
     sample = noise_ref[...].astype(jnp.float32)
     logr = jnp.sum(
@@ -336,7 +384,8 @@
             + ring_in[last - 1, cut].astype(jnp.float32)
         )
     collect(n, head_all, small_sems.at[3])
-    heads_ref[...] = head_all[...]
+    for j in range(n):
+        heads_ref[:, j * share : (j + 1) * share] = head_all[j]
     kept.wait()
     collect(n, out_ref, small_sems.at[7])
     collect(n, ordered, small_sems.at[6])
@@ -345,31 +394,41 @@
     collect(n, head_all, small_sems.at[2])
 
     def drain(step, _):
-        owner = mine(step)
+        for i in range(len(spans)):
+            gather_sib(step, i).wait_send()
+        for i in range(len(rung)):
+            @pl.when(step < last)
+            def _():
+                gather_copy(step + 1, i).wait_send()
+
         for i in range(len(cuts)):
             @pl.when(step < last)
             def _():
-                gather_copy(owner, step + 1, i).wait_send()
                 ring_copy(step, i).wait_send()
 
-            gather_sib(owner, step, i).wait_send()
+        if twinned:
+            @pl.when(step > 0)
+            def _():
+                gather_twin(step).wait_send()
+
         sib_copy(step).wait_send()
         return 0
 
     lax.fori_loop(0, r.ring, drain, 0)
 
 
-def step_call(n, x, weight, gain, gae, ret, slot, old_mean, noise, head, log_std):
+def step_call(n, groups, x, weight, gain, adv, slot, old_mean, noise, head, log_std):
     rows, width = x.shape
     shard = weight.shape[0]
     nact = log_std.shape[0]
     per = -(-(rows // n) // 8) * 8
     aligned = shard % 128 == 0
-    blocks = jnp.zeros((8, 128), jnp.bfloat16)
+    twinned = groups == 2 and shard % 64 == 0
+    blocks = []
     if not aligned:
         xf = x.astype(jnp.float32)
         normed = xf * lax.rsqrt(jnp.mean(xf * xf, -1, keepdims=True) + NORM_EPS) * gain
-        blocks = normed.astype(jnp.bfloat16).reshape(rows, n, shard).transpose(1, 0, 2)
+        blocks = [normed.astype(jnp.bfloat16).reshape(rows, n, shard).transpose(1, 0, 2)]
     count = len(pieces(shard))
     ring = n // 2
     share = width // n
@@ -377,19 +436,26 @@
     anywhere = pl.BlockSpec(memory_space=pl.ANY)
     sems = pltpu.SemaphoreType.DMA
     bf16, f32 = jnp.bfloat16, jnp.float32
+    fixed = functools.partial(step_kernel, n, nact, per, max(n // 4, 1), aligned, twinned)
+
+    def body(*refs):
+        given = 9
+        lhs = refs[given] if blocks else None
+        fixed(*refs[:given], lhs, *refs[given + len(blocks) :])
+
     return pl.pallas_call(
-        functools.partial(step_kernel, n, nact, per, max(n // 4, 1), aligned),
+        body,
         name="step",
         out_shape=(
             jax.ShapeDtypeStruct((n, per, width), bf16),
             jax.ShapeDtypeStruct((shard, width), f32),
-            jax.ShapeDtypeStruct((n, 16, share), f32),
+            jax.ShapeDtypeStruct((16, width), f32),
         ),
-        in_specs=[vmem, vmem, anywhere] + [vmem] * 8,
+        in_specs=[vmem, anywhere] + [vmem] * (7 + len(blocks)),
         out_specs=(anywhere, vmem, vmem),
         scratch_shapes=[
             pltpu.VMEM((rows, width) if aligned else (16, 128), bf16),
-            pltpu.VMEM((n, shard, width), bf16),
+            pltpu.VMEM((ring, 2 * shard, width), bf16),
             pltpu.VMEM((rows, width), f32),
             pltpu.VMEM((rows, width), bf16),
             pltpu.VMEM((rows, width), bf16),
@@ -410,10 +476,13 @@
             pltpu.VMEM((16, share), f32),
             pltpu.VMEM((n, 16, share), f32),
             sems((2,)),
-            sems((ring, count)),
-            sems((ring, count)),
-            sems((ring, count)),
-            sems((ring, count)),
+            sems((ring, 2 if twinned else 1)),
+            sems((ring, 2 if twinned else 1)),
+            sems((ring, 3 if twinned else 1)),
+            sems((ring, 3 if twinned else 1)),
+            sems((ring if twinned else 1,)),
+            sems((ring if twinned else 1,)),
+            pltpu.VMEM((48, width), bf16),
             sems((ring - 1, count)),
             sems((ring - 1, count)),
             sems((ring,)),
@@ -426,7 +495,7 @@
         cost_estimate=pl.CostEstimate(
             flops=4 * rows * width * width, bytes_accessed=32 * rows * width, transcendentals=0
         ),
-    )(x, blocks, weight, gain[None], gae, ret, slot, old_mean, noise, head, log_std[:, None])
+    )(x, weight, gain[None], adv, slot, old_mean, noise, head, log_std[None], *blocks)
 
 
 def advantages(reward, value_old, done):
@@ -462,14 +531,13 @@
     per_peer = local_rows // devices
     padded = -(-per_peer // 8) * 8
     slot = minibatch_perm // local_rows * padded + minibatch_perm % per_peer
-    head = jnp.pad(head_weight.T, ((0, 16 - head_weight.shape[1]), (0, 0)))
     moved, grad_weight, heads_all = step_call(
-        devices, obs_feat, out_weight, gain_in, gae[None], returns[None], slot[None],
-        old_mean.T, noise.T, jnp.tile(head, (3, 1)), log_std,
+        devices, lax.axis_size("groups"), obs_feat, out_weight, gain_in, jnp.stack([gae, returns]),
+        slot[None], old_mean.T, noise.T, head_weight.T, log_std,
     )
     hidden_out = moved[:, :per_peer].reshape(local_rows, width)
-    grad_head = heads_all[:, : nact + 1].swapaxes(0, 1).reshape(nact + 1, width).T
-    grad_std = heads_all[0, nact + 1, :nact]
+    grad_head = heads_all[: nact + 1].T
+    grad_std = heads_all[nact + 1, :nact]
     return (hidden_out, grad_weight, grad_head, grad_std)
 
 

time: 153 us -> 149 us (0.974)
  local copies, waits for them, and re-layouts: 12.1 us -> 7.41 us
    broadcast_in_dim x2 -> x0, local copies, waits for them, and re-layouts: 1.91 us -> none  [the longest x1 1.33 us: step_call(): log_std[:, None]]
    another operation x3 -> x2, local copies, waits for them, and re-layouts: 2.03 us -> 0.18 us  [local(): jnp.stack([gae, returns])]
    unnamed x6 -> x4, local copies, waits for them, and re-layouts: 4.5 us -> 3.79 us
where the time goes in v3:
time: 149 us; the launch traced here: 148 us
  Pallas kernels  137 us (92%)
  local copies, waits for them, and re-layouts  7.41 us (5%)
  other arithmetic  3.01 us (2%)
    pallas_call x1, Pallas kernels, step_call(): pl.pallas_call(body, name='step', out_shape=(jax.ShapeDtypeStruct((n, per...  137 us
    unnamed x4, local copies, waits for them, and re-layouts  3.79 us

profile of v3, /device:TPU:9, one launch (start us, length us, event | category | flops | bytes accessed | tf_op | source)
XLA Modules:
  0.0 148.2 jit_solution(12418802292320297403)
XLA Ops:
  0.6 0.7 fusion.47
  1.3 0.6 broadcast_in_dim.10.refs_4_
  1.9 0.8 add_subtract_fusion
  2.7 0.2 fusion.46
  2.9 0.1 stack.4
  3.0 0.1 stack_reshape.6
  3.1 0.7 slice_add_fusion
  3.8 0.1 stack_reshape.7
  3.9 0.6 pad_maximum_fusion.refs_3_
  4.5 137.1 %step.1 = (bf16[16,24,2048]{2,1,0:T(8,128)(2,1)}, f32[128,2048]{1,0:T(8,128)}, f32[16,2048]{1,0:T(8,128)}) custom-call(bf16[384,2048]{1,0:T(8,128)(2,1)} %refs_0_.1, bf16[128,2048]{1,0:T(8,128)(2,1)} %refs_1_.1, f32[1,2048]{1,0:T(1,128)} %bitcast.14, f32[2,384]{1,0:T(2,128)} %pad_maximum_fusion.refs_3_, s32[1,384]{1,0:T(1,128)} %broadcast_in_dim.10.refs_4_, ...), custom_call_target="tpu_custom_call" | custom-call | flops 6442450944 | bytes 25165824 | tf_op jit(solution)/shard_map/step/pallas_call | solution.py:446
  141.7 1.2 slice_bitcast_fusion.1
  142.8 1.6 %slice_bitcast_fusion = f32[2048,13]{0,1:T(8,128)} fusion(f32[16,2048]{1,0:T(8,128)} %get-tuple-element.9), kind=kLoop, calls=%fused_computation | loop fusion | bytes 212992 | tf_op jit(solution)/shard_map/transpose | solution.py:539
  144.4 0.0 copy-start
  144.4 2.8 %copy.17 = bf16[384,2048]{1,0:T(8,128)(2,1)} copy(bf16[384,2048]{1,0:T(8,128)(2,1)} %bitcast.10) | data formatting | bytes 3145728
  147.2 0.0 copy-done
  147.2 1.0 copy.18
Async XLA Ops:
  144.4 2.8 %copy-start = (f32[128,2048]{1,0:T(8,128)S(1)}, f32[128,2048]{1,0:T(8,128)}, u32[]{:S(2)}) copy-start(f32[128,2048]{1,0:T(8,128)} %get-tuple-element.41) | copy-start | bytes 3145732

commit v4 on v3

--- a/solution.py
+++ b/solution.py
@@ -436,7 +436,7 @@
     anywhere = pl.BlockSpec(memory_space=pl.ANY)
     sems = pltpu.SemaphoreType.DMA
     bf16, f32 = jnp.bfloat16, jnp.float32
-    fixed = functools.partial(step_kernel, n, nact, per, max(n // 4, 1), aligned, twinned)
+    fixed = functools.partial(step_kernel, n, nact, per, max(n // 2, 1), aligned, twinned)
 
     def body(*refs):
         given = 9

time: 149 us -> 147 us (0.987)
  Pallas kernels: 137 us -> 134 us
    pallas_call x1, Pallas kernels: 137 us -> 134 us  [step_call(): pl.pallas_call(body, name='step', out_shape=(jax.ShapeDtypeStruct((n, per...]
where the time goes in v4:
time: 147 us; the launch traced here: 145 us
  Pallas kernels  134 us (91%)
  local copies, waits for them, and re-layouts  7.41 us (5%)
  other arithmetic  3.01 us (2%)
    pallas_call x1, Pallas kernels, step_call(): pl.pallas_call(body, name='step', out_shape=(jax.ShapeDtypeStruct((n, per...  134 us
    unnamed x4, local copies, waits for them, and re-layouts  3.79 us

profile of v4, /device:TPU:9, one launch (start us, length us, event | category | flops | bytes accessed | tf_op | source)
XLA Modules:
  0.0 145.3 jit_solution(949776659650177330)
XLA Ops:
  0.6 0.7 fusion.47
  1.3 0.6 broadcast_in_dim.10.refs_4_
  1.9 0.8 add_subtract_fusion
  2.7 0.2 fusion.46
  2.9 0.1 stack.4
  3.0 0.1 stack_reshape.6
  3.1 0.7 slice_add_fusion
  3.8 0.1 stack_reshape.7
  3.9 0.6 pad_maximum_fusion.refs_3_
  4.5 134.3 %step.1 = (bf16[16,24,2048]{2,1,0:T(8,128)(2,1)}, f32[128,2048]{1,0:T(8,128)}, f32[16,2048]{1,0:T(8,128)}) custom-call(bf16[384,2048]{1,0:T(8,128)(2,1)} %refs_0_.1, bf16[128,2048]{1,0:T(8,128)(2,1)} %refs_1_.1, f32[1,2048]{1,0:T(1,128)} %bitcast.14, f32[2,384]{1,0:T(2,128)} %pad_maximum_fusion.refs_3_, s32[1,384]{1,0:T(1,128)} %broadcast_in_dim.10.refs_4_, ...), custom_call_target="tpu_custom_call" | custom-call | flops 6442450944 | bytes 25165824 | tf_op jit(solution)/shard_map/step/pallas_call | solution.py:446
  138.8 1.2 slice_bitcast_fusion.1
  140.0 1.6 %slice_bitcast_fusion = f32[2048,13]{0,1:T(8,128)} fusion(f32[16,2048]{1,0:T(8,128)} %get-tuple-element.9), kind=kLoop, calls=%fused_computation | loop fusion | bytes 212992 | tf_op jit(solution)/shard_map/transpose | solution.py:539
  141.5 0.0 copy-start
  141.5 2.8 %copy.17 = bf16[384,2048]{1,0:T(8,128)(2,1)} copy(bf16[384,2048]{1,0:T(8,128)(2,1)} %bitcast.10) | data formatting | bytes 3145728
  144.4 0.0 copy-done
  144.4 1.0 copy.18
Async XLA Ops:
  141.5 2.8 %copy-start = (f32[128,2048]{1,0:T(8,128)S(1)}, f32[128,2048]{1,0:T(8,128)}, u32[]{:S(2)}) copy-start(f32[128,2048]{1,0:T(8,128)} %get-tuple-element.41) | copy-start | bytes 3145732
